TPU v7x, 128 devices: a whole 4x4x4 slice. The times are simulated.
128 devices in a mesh: comp: 2 (over z_hi), mr: 64 (over z_lo, y, x, core).
Axes of the slice: x: 4, y: 4, z: 4 (z_hi: 2, z_lo: 2; z = z_hi * 2 + z_lo), core: 2. Of those that a mesh axis runs over, the one named last changes fastest.
Arguments:
- spectrum: float32 [2, 1024, 2, 64, 512], P('comp', 'mr'), may hold values from -6 to 6
- radial_basis: bfloat16 [1024, 1024, 512], P('mr'), may hold values from -0.25 to 0.25
- cutoff: int32 [1024], P('mr'), may hold values from 128 to 512, as said below
- couplings: float32 [2, 2], replicated, may hold values from 0.5 to 1.5
- trap_potential: float32 [1024], replicated, may hold values from 0 to 2
- weights: float32 [1024], replicated, may hold values from 0.25 to 0.75
Outputs:
- evolved: float32 [2, 1024, 2, 64, 512], P('comp', 'mr')
Inputs may be any that keep to these rules, and one draw needn't show every extreme that they name: cutoff[m] is the number of Laguerre degrees kept for angular mode m; degrees from cutoff[m] on are dropped.
All inputs are finite; a program needn't handle non-finite values.
Results may differ from a plain program's by a relative error of at most 0.0089.
Values may be sent and summed in bfloat16 or wider, within the bound.
A program may use at most 128 MiB of HBM per device.

v0:
```python
import math

import jax
import jax.numpy as jnp
from jax import lax
from jax.sharding import PartitionSpec as P

TIMESTEP = 0.5
ROTATION = 0.7


def from_partner(x, axis, stride):
    return lax.ppermute(x, axis, [(i, i ^ 1 << stride) for i in range(lax.axis_size(axis))])


def spectral_tables(mode_total):
    ordinal = jnp.arange(mode_total, dtype=jnp.int32)
    product = ordinal[:, None] * ordinal[None, :] % mode_total
    angles = product.astype(jnp.float32) * (2.0 * math.pi / mode_total)
    normalizer = 1.0 / math.sqrt(mode_total)
    return (
        (jnp.cos(angles) * normalizer).astype(jnp.bfloat16),
        (jnp.sin(angles) * normalizer).astype(jnp.bfloat16),
    )


def rotate(real_part, imag_part, phase_angle):
    cosine = jnp.cos(phase_angle)
    sine_value = jnp.sin(phase_angle)
    return (
        real_part * cosine + imag_part * sine_value,
        imag_part * cosine - real_part * sine_value,
    )


def forward_modes(cosine_table, sine_table, radial, planes):
    cosine_term = jnp.einsum(
        "am,rmk->rak", cosine_table, radial, preferred_element_type=jnp.float32
    )
    sine_term = jnp.einsum("am,rmk->rak", sine_table, radial, preferred_element_type=jnp.float32)
    real_part = cosine_term[..., :planes] - sine_term[..., planes:]
    imag_part = sine_term[..., :planes] + cosine_term[..., planes:]
    return (real_part, imag_part)


def inverse_modes(cosine_table, sine_table, kicked, planes):
    cosine_back = jnp.einsum(
        "am,rak->rmk", cosine_table, kicked, preferred_element_type=jnp.float32
    )
    sine_back = jnp.einsum("am,rak->rmk", sine_table, kicked, preferred_element_type=jnp.float32)
    back_real = cosine_back[..., :planes] + sine_back[..., planes:]
    back_imag = cosine_back[..., planes:] - sine_back[..., :planes]
    return jnp.concatenate([back_real, back_imag], -1)


def on_device(spectrum, radial_basis, cutoff, couplings, trap_potential, weights):
    local_modes = spectrum.shape[1]
    planes = spectrum.shape[3]
    degrees = spectrum.shape[4]
    radius_count = radial_basis.shape[1]
    mode_width = lax.axis_size("mr")
    mode_total = local_modes * mode_width
    first_mode = lax.axis_index("mr") * local_modes
    mode_ids = first_mode + jnp.arange(local_modes, dtype=jnp.int32)
    signed = jnp.where(mode_ids < mode_total // 2, mode_ids, mode_ids - mode_total).astype(
        jnp.float32
    )
    degree_ids = jnp.arange(degrees, dtype=jnp.int32)
    energy = (
        2.0 * degree_ids.astype(jnp.float32)[None, :]
        + (jnp.abs(signed) + 1.0 - ROTATION * signed)[:, None]
    )
    kinetic_phase = TIMESTEP * energy
    kept_mask = (degree_ids[None, :] < cutoff[:, None]).astype(jnp.float32)
    spin_real, spin_imag = rotate(spectrum[0, :, 0], spectrum[0, :, 1], kinetic_phase[:, None, :])
    coeffs = jnp.concatenate(
        [spin_real * kept_mask[:, None, :], spin_imag * kept_mask[:, None, :]], axis=1
    ).astype(jnp.bfloat16)
    synthesized = jnp.einsum(
        "mkn,mrn->rmk", coeffs, radial_basis, preferred_element_type=jnp.float32
    ).astype(jnp.bfloat16)
    cosine_table, sine_table = spectral_tables(mode_total)
    row_count = radius_count // mode_width
    first_row = lax.axis_index("mr") * row_count
    trap_rows = lax.dynamic_slice_in_dim(trap_potential, first_row, row_count)
    weight_rows = lax.dynamic_slice_in_dim(weights, first_row, row_count)
    radial = lax.all_to_all(synthesized, "mr", split_axis=0, concat_axis=1, tiled=True)
    real_part, imag_part = forward_modes(cosine_table, sine_table, radial, planes)
    density = real_part * real_part + imag_part * imag_part
    partner = from_partner(density, "comp", 0)
    component = lax.axis_index("comp")
    strength = lax.dynamic_index_in_dim(couplings, component, 0, keepdims=False)
    phase_angle = TIMESTEP * (
        strength[0] * density + strength[1] * partner + trap_rows[:, None, None]
    )
    kick_real, kick_imag = rotate(real_part, imag_part, phase_angle)
    kicked = jnp.concatenate([kick_real, kick_imag], -1).astype(jnp.bfloat16)
    analysis_input = (
        inverse_modes(cosine_table, sine_table, kicked, planes) * weight_rows[:, None, None]
    ).astype(jnp.bfloat16)
    gathered_modes = lax.all_to_all(analysis_input, "mr", split_axis=1, concat_axis=0, tiled=True)
    evolved = (
        jnp.einsum("rmk,mrn->mkn", gathered_modes, radial_basis, preferred_element_type=jnp.float32)
        * kept_mask[:, None, :]
    )
    return evolved.reshape(1, local_modes, 2, planes, degrees)


def solution(mesh):
    in_specs = (P("comp", "mr", None, None, None), P("mr", None, None), P("mr"), P(), P(), P())
    out_specs = P("comp", "mr", None, None, None)
    return jax.shard_map(
        on_device, mesh=mesh, in_specs=in_specs, out_specs=out_specs, check_vma=False
    )
```

profile of v0, /device:TPU:1, one launch (start us, length us, event | category | flops | bytes accessed | tf_op | source)
XLA Modules:
  0.0 388.5 jit_solution(9481034302977023700)
XLA Ops:
  0.0 0.0 copy-start
  0.0 0.7 fusion.28
  0.8 0.2 fusion.27
  1.0 2.9 fusion.16
  3.9 17.4 %convert_bitcast_fusion = bf16[1024,16,128]{0,2,1:T(8,128)(2,1)} fusion(bf16[16,1024,512]{2,1,0:T(8,128)(2,1)} %param.7, bf16[16,64,512]{2,1,0:T(8,128)(2,1)S(1)} %get-tuple-element.10, bf16[16,64,512]{2,1,0:T(8,128)(2,1)S(1)} %get-tuple-element.9), kind=kOutput, calls=%fused_computation.23 | convolution fusion | flops 2153775104 | bytes 23068672 | tf_op jit(solution)/shard_map/mkn,mrn->rmk/dot_general | solution.py:79
  21.3 6.9 %copy.22 = bf16[1024,16,128]{2,1,0:T(8,128)(2,1)} copy(bf16[1024,16,128]{0,2,1:T(8,128)(2,1)} %convert_bitcast_fusion) | data formatting | bytes 8388608 | tf_op jit(solution)/shard_map/convert_element_type | solution.py:81
  28.2 62.0 %all_to_all.36 = bf16[1024,16,128]{2,1,0:T(8,128)(2,1)S(1)} all-to-all(bf16[1024,16,128]{2,1,0:T(8,128)(2,1)} %copy.22), channel_id=1, replica_groups=mesh['comp'=2,'mr'=64] {'mr'}, dimensions={0} | all-to-all | bytes 8388608 | tf_op jit(solution)/shard_map/all_to_all | solution.py:87
  90.3 1.1 copy.23
  91.4 21.3 %convolution_bitcast_fusion.2 = f32[16,1024,128]{1,2,0:T(8,128)S(1)} fusion(bf16[16,1024,128]{2,1,0:T(8,128)(2,1)S(1)} %bitcast.62), kind=kOutput, calls=%fused_computation.27 | convolution fusion | flops 4311744512 | bytes 12582912 | tf_op jit(solution)/shard_map/am,rmk->rak/dot_general | solution.py:40
  112.7 0.0 copy-start.2
  112.7 21.3 %convolution_bitcast_fusion.3 = f32[16,1024,128]{1,2,0:T(8,128)S(1)} fusion(bf16[16,1024,128]{2,1,0:T(8,128)(2,1)S(1)} %bitcast.63), kind=kOutput, calls=%fused_computation.28 | convolution fusion | flops 4311744512 | bytes 12582912 | tf_op jit(solution)/shard_map/am,rmk->rak/dot_general | solution.py:37
  134.0 0.0 copy-done.2
  134.0 0.0 copy-start.3
  134.0 4.0 %multiply_add_fusion = f32[16,1024,64]{1,2,0:T(8,128)} fusion(f32[16,1024,128]{1,2,0:T(8,128)S(1)} %convolution_bitcast_fusion.2, f32[16,1024,128]{1,2,0:T(8,128)S(1)} %convolution_bitcast_fusion.3), kind=kLoop, calls=%fused_computation.18 | loop fusion | flops 5242880 | bytes 20971520 | tf_op jit(solution)/shard_map/add | solution.py:89
  138.1 0.6 copy-done.3
  138.6 3.3 collective-permute-start
  142.0 0.8 dynamic_slice.11
  142.7 0.8 dynamic_slice.12
  143.5 0.0 copy-done
  143.5 0.6 fusion.55
  144.1 88.6 %collective-permute-done = f32[16,1024,64]{1,2,0:T(8,128)} collective-permute-done((f32[16,1024,64]{1,2,0:T(8,128)}, f32[16,1024,64]{1,2,0:T(8,128)}, u32[]{:S(2)}, u32[]{:S(2)}) %collective-permute-start) | collective-permute-done | bytes 4194336 | tf_op jit(solution)/shard_map/ppermute | solution.py:13
  232.7 21.6 %add_convert_fusion = (bf16[16,1024,64]{1,2,0:T(8,128)(2,1)S(1)}, bf16[16,1024,64]{1,2,0:T(8,128)(2,1)S(1)}) fusion(f32[16]{0:T(128)S(1)} %dynamic_slice.11, f32[16,1024,64]{1,2,0:T(8,128)} %collective-permute-done, f32[]{:T(128)} %bitcast.11, f32[]{:T(128)} %bitcast.10, f32[16,1024,128]{1,2,0:T(8,128)} %copy-done.2, f32[16,1024,128]{1,2,0:T(8,128)} %copy-done.3), kind=kLoop, calls=%fused_computation.16 | loop fusion | flops 18874368 | bytes 25165896 | tf_op jit(solution)/shard_map/convert
  254.3 21.2 %convolution_bitcast_fusion.1 = f32[16,1024,128]{1,2,0:T(8,128)} fusion(bf16[16,1024,64]{1,2,0:T(8,128)(2,1)S(1)} %get-tuple-element.6, bf16[16,1024,64]{1,2,0:T(8,128)(2,1)S(1)} %get-tuple-element.5), kind=kOutput, calls=%fused_computation.26 | convolution fusion | flops 4320133120 | bytes 12582912 | tf_op jit(solution)/shard_map/am,rak->rmk/dot_general | solution.py:47
  275.5 21.3 %convolution_bitcast_fusion = f32[16,1024,128]{1,2,0:T(8,128)} fusion(bf16[16,1024,64]{1,2,0:T(8,128)(2,1)S(1)} %get-tuple-element.6, bf16[16,1024,64]{1,2,0:T(8,128)(2,1)S(1)} %get-tuple-element.5), kind=kOutput, calls=%fused_computation.25 | convolution fusion | flops 4320133120 | bytes 12582912 | tf_op jit(solution)/shard_map/am,rak->rmk/dot_general | solution.py:50
  296.8 10.6 %slice_add_fusion = (f32[16,1024,64]{1,2,0:T(8,128)S(1)}, f32[16,1024,64]{1,2,0:T(8,128)}) fusion(f32[16,1024,128]{1,2,0:T(8,128)} %convolution_bitcast_fusion, f32[16,1024,128]{1,2,0:T(8,128)} %convolution_bitcast_fusion.1), kind=kLoop, calls=%fused_computation.9 | loop fusion | flops 2097152 | bytes 25165824 | tf_op jit(solution)/shard_map/add | solution.py:51
  307.4 4.2 %fusion = bf16[16,1024,128]{1,2,0:T(8,128)(2,1)} fusion(f32[16,1024,64]{1,2,0:T(8,128)} %get-tuple-element.8, f32[16,1024,64]{1,2,0:T(8,128)S(1)} %get-tuple-element.7, f32[16]{0:T(128)S(1)} %dynamic_slice.12), kind=kLoop, calls=%fused_computation.1 | loop fusion | flops 6291456 | bytes 12582976 | tf_op jit(solution)/shard_map/convert_element_type | solution.py:100
  311.6 6.8 %copy.26 = bf16[16,1024,128]{2,0,1:T(8,128)(2,1)} copy(bf16[16,1024,128]{1,2,0:T(8,128)(2,1)} %fusion) | data formatting | bytes 8388608 | tf_op jit(solution)/shard_map/convert_element_type | solution.py:100
  318.4 57.6 %all_to_all.37 = bf16[16,1024,128]{2,0,1:T(8,128)(2,1)S(1)} all-to-all(bf16[16,1024,128]{2,0,1:T(8,128)(2,1)} %copy.26), channel_id=1, replica_groups=mesh['comp'=2,'mr'=64] {'mr'}, dimensions={1} | all-to-all | bytes 8388608 | tf_op jit(solution)/shard_map/all_to_all | solution.py:101
  376.0 1.1 copy.28
  377.1 0.0 copy-start.1
  377.1 11.0 %broadcast_multiply_fusion = f32[16,128,512]{2,1,0:T(8,128)} fusion(f32[16,512]{1,0:T(8,128)S(1)} %fusion.28, bf16[16,1024,512]{2,1,0:T(8,128)(2,1)} %param.7, bf16[1024,16,128]{2,1,0:T(8,128)(2,1)S(1)} %bitcast.59), kind=kOutput, calls=%fused_computation.44 | convolution fusion | flops 2148532224 | bytes 25198592 | tf_op jit(solution)/shard_map/rmk,mrn->mkn/dot_general | solution.py:103
  388.1 0.0 copy-done.1
  (3 shorter events, 0.0 us)
Async XLA Ops:
  0.0 143.5 %copy-start = (f32[2,2]{1,0:T(2,128)S(1)}, f32[2,2]{1,0:T(2,128)}, u32[]{:S(2)}) copy-start(f32[2,2]{1,0:T(2,128)} %param.9) | copy-start | bytes 52
  112.7 21.3 %copy-start.2 = (f32[16,1024,128]{1,2,0:T(8,128)}, f32[16,1024,128]{1,2,0:T(8,128)S(1)}, u32[]{:S(2)}) copy-start(f32[16,1024,128]{1,2,0:T(8,128)S(1)} %convolution_bitcast_fusion.2) | copy-start | bytes 25165828
  134.0 4.6 %copy-start.3 = (f32[16,1024,128]{1,2,0:T(8,128)}, f32[16,1024,128]{1,2,0:T(8,128)S(1)}, u32[]{:S(2)}) copy-start(f32[16,1024,128]{1,2,0:T(8,128)S(1)} %convolution_bitcast_fusion.3) | copy-start | bytes 25165828
  138.6 94.0 %collective-permute-start = (f32[16,1024,64]{1,2,0:T(8,128)}, f32[16,1024,64]{1,2,0:T(8,128)}, u32[]{:S(2)}, u32[]{:S(2)}) collective-permute-start(f32[16,1024,64]{1,2,0:T(8,128)} %multiply_add_fusion), channel_id=1, source_target_pairs={{0,64},{64,0},{1,65},{65,1},{2,66},{66,2},{3,67},{67,3},{4,68},{68... | collective-permute-start | bytes 12582920 | tf_op jit(solution)/shard_map/ppermute | solution.py:13
  377.1 11.0 %copy-start.1 = (f32[2,2]{1,0:T(2,128)S(1)}, f32[2,2]{1,0:T(2,128)}, u32[]{:S(2)}) copy-start(f32[2,2]{1,0:T(2,128)} %param.9) | copy-start | bytes 52
where the time goes:
time: 393 us; the launch traced here: 389 us
  blocking collectives  120 us (31%)
  matrix products  114 us (29%)
  waiting for transfers between devices  88.6 us (23%)
  other arithmetic  44.3 us (11%)
  local copies, waits for them, and re-layouts  18.6 us (5%)
    ppermute x1, waiting for transfers between devices, from_partner(): lax.ppermute(x, axis, [(i, i ^ 1 << stride) for i in range(lax.axis_size(...  88.6 us
    all_to_all x1, blocking collectives, on_device(): lax.all_to_all(synthesized, 'mr', split_axis=0, concat_axis=1, tiled=True)  62 us
    all_to_all x1, blocking collectives, on_device(): lax.all_to_all(analysis_input, 'mr', split_axis=1, concat_axis=0, tiled=T...  57.6 us
    another operation x2, other arithmetic  24.6 us
    dot_general x1, matrix products, forward_modes(): jnp.einsum('am,rmk->rak', sine_table, radial, preferred_element_type=jnp....  21.3 us
    dot_general x1, matrix products, forward_modes(): jnp.einsum('am,rmk->rak', cosine_table, radial, preferred_element_type=jn...  21.3 us
    dot_general x1, matrix products, inverse_modes(): jnp.einsum('am,rak->rmk', sine_table, kicked, preferred_element_type=jnp....  21.3 us
    dot_general x1, matrix products, inverse_modes(): jnp.einsum('am,rak->rmk', cosine_table, kicked, preferred_element_type=jn...  21.2 us
  transfers between devices with their start and end apart: 1, of which 1 were waited for; matrix products, arithmetic and copies ran while one was open for 1% of the time, Pallas kernels for 0%

commit v1 on v0

--- a/solution.py
+++ b/solution.py
@@ -7,10 +7,6 @@
 
 TIMESTEP = 0.5
 ROTATION = 0.7
-
-
-def from_partner(x, axis, stride):
-    return lax.ppermute(x, axis, [(i, i ^ 1 << stride) for i in range(lax.axis_size(axis))])
 
 
 def spectral_tables(mode_total):
@@ -80,25 +76,31 @@
         "mkn,mrn->rmk", coeffs, radial_basis, preferred_element_type=jnp.float32
     ).astype(jnp.bfloat16)
     cosine_table, sine_table = spectral_tables(mode_total)
-    row_count = radius_count // mode_width
-    first_row = lax.axis_index("mr") * row_count
+    comp_width = lax.axis_size("comp")
+    row_count = radius_count // (mode_width * comp_width)
+    first_row = (lax.axis_index("comp") * mode_width + lax.axis_index("mr")) * row_count
     trap_rows = lax.dynamic_slice_in_dim(trap_potential, first_row, row_count)
     weight_rows = lax.dynamic_slice_in_dim(weights, first_row, row_count)
-    radial = lax.all_to_all(synthesized, "mr", split_axis=0, concat_axis=1, tiled=True)
+    everyone = ("comp", "mr")
+    radial = lax.all_to_all(synthesized, everyone, split_axis=0, concat_axis=1, tiled=True)
+    radial = radial.reshape(row_count * comp_width, mode_total, 2 * planes)
     real_part, imag_part = forward_modes(cosine_table, sine_table, radial, planes)
-    density = real_part * real_part + imag_part * imag_part
-    partner = from_partner(density, "comp", 0)
-    component = lax.axis_index("comp")
-    strength = lax.dynamic_index_in_dim(couplings, component, 0, keepdims=False)
+    density = (real_part * real_part + imag_part * imag_part).reshape(
+        row_count, comp_width, mode_total, planes
+    )
     phase_angle = TIMESTEP * (
-        strength[0] * density + strength[1] * partner + trap_rows[:, None, None]
+        couplings[:, 0][None, :, None, None] * density
+        + couplings[:, 1][None, :, None, None] * density[:, ::-1]
+        + trap_rows[:, None, None, None]
     )
-    kick_real, kick_imag = rotate(real_part, imag_part, phase_angle)
+    kick_real, kick_imag = rotate(real_part, imag_part, phase_angle.reshape(real_part.shape))
     kicked = jnp.concatenate([kick_real, kick_imag], -1).astype(jnp.bfloat16)
-    analysis_input = (
-        inverse_modes(cosine_table, sine_table, kicked, planes) * weight_rows[:, None, None]
-    ).astype(jnp.bfloat16)
-    gathered_modes = lax.all_to_all(analysis_input, "mr", split_axis=1, concat_axis=0, tiled=True)
+    back = inverse_modes(cosine_table, sine_table, kicked, planes)
+    back = back.reshape(row_count, comp_width * mode_total, 2 * planes)
+    analysis_input = (back * weight_rows[:, None, None]).astype(jnp.bfloat16)
+    gathered_modes = lax.all_to_all(
+        analysis_input, everyone, split_axis=1, concat_axis=0, tiled=True
+    )
     evolved = (
         jnp.einsum("rmk,mrn->mkn", gathered_modes, radial_basis, preferred_element_type=jnp.float32)
         * kept_mask[:, None, :]

time: 393 us -> 324 us (0.82)
  blocking collectives: 120 us -> 57.1 us
  waiting for transfers between devices: 88.6 us -> 50.7 us
  local copies, waits for them, and re-layouts: 18.6 us -> 34.1 us
  starting transfers between devices: 3.3 us -> 12.7 us
  other arithmetic: 44.3 us -> 48.3 us
    ppermute x1 -> x0, waiting for transfers between devices: 88.6 us -> none  [from_partner(): lax.ppermute(x, axis, [(i, i ^ 1 << stride) for i in range(lax.axis_size(...]
    all_to_all x2 -> x1, blocking collectives: 120 us -> 57.1 us  [on_device(): lax.all_to_all(analysis_input, everyone, split_axis=1, concat_axis=0, til...]
    all_to_all x0 -> x1, waiting for transfers between devices: none -> 50.7 us  [on_device(): lax.all_to_all(synthesized, everyone, split_axis=0, concat_axis=1, tiled=...]
    another operation x2, other arithmetic: 24.6 us -> 8.4 us
    cos x1 -> x2, other arithmetic: 0.2 us -> 15.5 us  [rotate(): cosine = jnp.cos(phase_angle)]
    all_to_all x0 -> x1, starting transfers between devices: none -> 12.7 us  [on_device(): lax.all_to_all(synthesized, everyone, split_axis=0, concat_axis=1, tiled=...]
    concatenate x0 -> x1, local copies, waits for them, and re-layouts: none -> 9.24 us  [inverse_modes(): return jnp.concatenate([back_real, back_imag], -1)]
    concatenate x0 -> x1, other arithmetic: none -> 6.79 us  [inverse_modes(): return jnp.concatenate([back_real, back_imag], -1)]
where the time goes in v1:
time: 324 us; the launch traced here: 320 us
  matrix products  116 us (36%)
  blocking collectives  57.1 us (18%)
  waiting for transfers between devices  50.7 us (16%)
  other arithmetic  48.3 us (15%)
  local copies, waits for them, and re-layouts  34.1 us (11%)
  starting transfers between devices  12.7 us (4%)
    all_to_all x1, blocking collectives, on_device(): lax.all_to_all(analysis_input, everyone, split_axis=1, concat_axis=0, til...  57.1 us
    all_to_all x1, waiting for transfers between devices, on_device(): lax.all_to_all(synthesized, everyone, split_axis=0, concat_axis=1, tiled=...  50.7 us
    dot_general x1, matrix products, inverse_modes(): jnp.einsum('am,rak->rmk', sine_table, kicked, preferred_element_type=jnp....  23.9 us
    dot_general x1, matrix products, forward_modes(): jnp.einsum('am,rmk->rak', sine_table, radial, preferred_element_type=jnp....  21.4 us
    dot_general x1, matrix products, forward_modes(): jnp.einsum('am,rmk->rak', cosine_table, radial, preferred_element_type=jn...  21.3 us
    dot_general x1, matrix products, inverse_modes(): jnp.einsum('am,rak->rmk', cosine_table, kicked, preferred_element_type=jn...  21.3 us
    dot_general x1, matrix products, on_device(): jnp.einsum('mkn,mrn->rmk', coeffs, radial_basis, preferred_element_type=j...  17.4 us
    cos x2, other arithmetic, rotate(): cosine = jnp.cos(phase_angle)  15.5 us
  transfers between devices with their start and end apart: 1, of which 1 were waited for; matrix products, arithmetic and copies ran while one was open for 1% of the time, Pallas kernels for 0%

profile of v1, /device:TPU:1, one launch (start us, length us, event | category | flops | bytes accessed | tf_op | source)
XLA Modules:
  0.0 319.5 jit_solution(5036196517199933014)
XLA Ops:
  0.0 0.7 fusion.34
  0.7 0.2 fusion.33
  0.9 3.0 fusion.22
  4.0 17.4 %convert_bitcast_fusion = bf16[1024,16,128]{0,2,1:T(8,128)(2,1)} fusion(bf16[16,1024,512]{2,1,0:T(8,128)(2,1)} %param.7, bf16[16,64,512]{2,1,0:T(8,128)(2,1)S(1)} %get-tuple-element.12, bf16[16,64,512]{2,1,0:T(8,128)(2,1)S(1)} %get-tuple-element.11), kind=kOutput, calls=%fused_computation.30 | convolution fusion | flops 2153775104 | bytes 23068672 | tf_op jit(solution)/shard_map/mkn,mrn->rmk/dot_general | solution.py:75
  21.3 6.9 %copy.20 = bf16[1024,16,128]{2,1,0:T(8,128)(2,1)} copy(bf16[1024,16,128]{0,2,1:T(8,128)(2,1)} %convert_bitcast_fusion) | data formatting | bytes 8388608 | tf_op jit(solution)/shard_map/convert_element_type | solution.py:77
  28.2 0.0 copy-start.2
  28.2 12.7 %all-to-all-start = ((bf16[1024,16,128]{2,1,0:T(8,128)(2,1)}), bf16[1024,16,128]{2,1,0:T(8,128)(2,1)}, u32[]{:S(2)}, u32[]{:S(2)}) async-start(bf16[1024,16,128]{2,1,0:T(8,128)(2,1)} %copy.20), calls=%async_computation | async-start | bytes 8388608 | tf_op jit(solution)/shard_map/all_to_all | solution.py:85
  40.9 0.8 dynamic_slice.6
  41.7 0.8 dynamic_slice.7
  42.4 0.0 copy-done.2
  42.4 0.2 slice_reduce_fusion.1
  42.6 50.7 %all-to-all-done = bf16[1024,16,128]{2,1,0:T(8,128)(2,1)} async-done(((bf16[1024,16,128]{2,1,0:T(8,128)(2,1)}), bf16[1024,16,128]{2,1,0:T(8,128)(2,1)}, u32[]{:S(2)}, u32[]{:S(2)}) %all-to-all-start) | async-done | bytes 4194336 | tf_op jit(solution)/shard_map/all_to_all | solution.py:85
  93.3 2.9 copy.21
  96.3 21.4 %convolution_bitcast_fusion.2 = f32[16,1024,128]{1,2,0:T(8,128)S(1)} fusion(bf16[16,1024,128]{2,1,0:T(8,128)(2,1)S(1)} %bitcast.85), kind=kOutput, calls=%fused_computation.34 | convolution fusion | flops 4311744512 | bytes 12582912 | tf_op jit(solution)/shard_map/am,rmk->rak/dot_general | solution.py:36
  117.7 21.3 %convolution_bitcast_fusion.3 = f32[16,1024,128]{1,2,0:T(8,128)S(1)} fusion(bf16[16,1024,128]{2,1,0:T(8,128)(2,1)S(1)} %bitcast.86), kind=kOutput, calls=%fused_computation.35 | convolution fusion | flops 4311744512 | bytes 12582912 | tf_op jit(solution)/shard_map/am,rmk->rak/dot_general | solution.py:33
  139.0 2.2 multiply_add_fusion
  141.2 15.3 %fusion.14 = (f32[8,2,1024,64]{2,3,1,0:T(8,128)S(1)}, f32[8,2,1024,64]{2,3,1,0:T(8,128)S(1)}) fusion(f32[8,2,1024,64]{2,3,1,0:T(8,128)S(1)} %bitcast.83, f32[8]{0:T(128)S(1)} %dynamic_slice.6, f32[2]{0:T(128)S(1)} %get-tuple-element.6, f32[2]{0:T(128)S(1)} %get-tuple-element.5), kind=kLoop, calls=%fused_computation.37 | loop fusion | flops 5242880 | bytes 12582960 | tf_op jit(solution)/shard_map/cos | solution.py:24
  156.5 5.4 %fusion.5 = (bf16[16,1024,64]{1,2,0:T(8,128)(2,1)}, bf16[16,1024,64]{1,2,0:T(8,128)(2,1)}) fusion(f32[8,2,1024,64]{2,3,1,0:T(8,128)S(1)} %get-tuple-element.14, f32[8,2,1024,64]{2,3,1,0:T(8,128)S(1)} %get-tuple-element.13, f32[16,1024,128]{1,2,0:T(8,128)S(1)} %convolution_bitcast_fusion.2, f32[16,1024,128]{1,2,0:T(8,128)S(1)} %convolution_bitcast_fusion.3), kind=kLoop, calls=%fused_computation.17 | loop fusion | flops 10485760 | bytes 29360128 | tf_op jit(solution)/shard_map/convert
  161.9 0.0 copy-start
  161.9 0.0 copy-start.1
  161.9 23.9 %convolution_bitcast_fusion = f32[16,1024,128]{1,2,0:T(8,128)} fusion(bf16[16,1024,64]{1,2,0:T(8,128)(2,1)} %get-tuple-element.8, bf16[16,1024,64]{1,2,0:T(8,128)(2,1)} %get-tuple-element.7), kind=kOutput, calls=%fused_computation.32 | convolution fusion | flops 4320133120 | bytes 12582912 | tf_op jit(solution)/shard_map/am,rak->rmk/dot_general | solution.py:46
  185.8 0.0 copy-done
  185.8 0.0 copy-done.1
  185.8 21.3 %convolution_bitcast_fusion.1 = f32[16,1024,128]{1,2,0:T(8,128)} fusion(bf16[16,1024,64]{1,2,0:T(8,128)(2,1)S(1)} %copy-done.1, bf16[16,1024,64]{1,2,0:T(8,128)(2,1)S(1)} %copy-done), kind=kOutput, calls=%fused_computation.33 | convolution fusion | flops 4320133120 | bytes 12582912 | tf_op jit(solution)/shard_map/am,rak->rmk/dot_general | solution.py:43
  207.1 10.6 %slice_add_fusion = (f32[16,1024,64]{1,2,0:T(8,128)S(1)}, f32[16,1024,64]{1,2,0:T(8,128)}) fusion(f32[16,1024,128]{1,2,0:T(8,128)} %convolution_bitcast_fusion, f32[16,1024,128]{1,2,0:T(8,128)} %convolution_bitcast_fusion.1), kind=kLoop, calls=%fused_computation.10 | loop fusion | flops 2097152 | bytes 25165824 | tf_op jit(solution)/shard_map/add | solution.py:47
  217.7 6.8 %pad_maximum_fusion = f32[16,1024,128]{1,2,0:T(8,128)} fusion(f32[16,1024,64]{1,2,0:T(8,128)} %get-tuple-element.10, f32[16,1024,64]{1,2,0:T(8,128)S(1)} %get-tuple-element.9), kind=kLoop, calls=%fused_computation | loop fusion | flops 2097152 | bytes 16777216 | tf_op jit(solution)/shard_map/concatenate | solution.py:49
  224.4 9.2 %copy.24 = f32[16,1024,128]{2,1,0:T(8,128)} copy(f32[16,1024,128]{1,2,0:T(8,128)} %pad_maximum_fusion) | data formatting | bytes 16777216 | tf_op jit(solution)/shard_map/concatenate | solution.py:49
  233.7 4.1 %fusion = bf16[8,2048,128]{2,1,0:T(8,128)(2,1)S(1)} fusion(f32[8]{0:T(128)S(1)} %dynamic_slice.7, f32[8,2048,128]{2,1,0:T(8,128)} %bitcast.81), kind=kLoop, calls=%fused_computation.2 | loop fusion | flops 4194304 | bytes 12582944 | tf_op jit(solution)/shard_map/convert_element_type | solution.py:100
  237.8 11.9 %copy.25 = bf16[8,2048,128]{2,0,1:T(8,128)(2,1)S(1)} copy(bf16[8,2048,128]{2,1,0:T(8,128)(2,1)S(1)} %fusion) | data formatting | bytes 8388608 | tf_op jit(solution)/shard_map/convert_element_type | solution.py:100
  249.8 57.1 %all_to_all.33 = bf16[8,2048,128]{2,0,1:T(8,128)(2,1)S(1)} all-to-all(bf16[8,2048,128]{2,0,1:T(8,128)(2,1)S(1)} %copy.25), channel_id=1, replica_groups=mesh['comp'=2,'mr'=64] {'comp','mr'}, dimensions={1} | all-to-all | bytes 8388608 | tf_op jit(solution)/shard_map/all_to_all | solution.py:101
  306.9 1.4 copy.27
  308.3 11.0 %broadcast_multiply_fusion = f32[16,128,512]{2,1,0:T(8,128)} fusion(f32[16,512]{1,0:T(8,128)S(1)} %fusion.34, bf16[16,1024,512]{2,1,0:T(8,128)(2,1)} %param.7, bf16[1024,16,128]{2,1,0:T(8,128)(2,1)S(1)} %bitcast.82), kind=kOutput, calls=%fused_computation.53 | convolution fusion | flops 2148532224 | bytes 25198592 | tf_op jit(solution)/shard_map/rmk,mrn->mkn/dot_general | solution.py:105
  (2 shorter events, 0.0 us)
Async XLA Ops:
  28.2 14.2 %copy-start.2 = (f32[2,2]{1,0:T(2,128)S(1)}, f32[2,2]{1,0:T(2,128)}, u32[]{:S(2)}) copy-start(f32[2,2]{1,0:T(2,128)} %param.9) | copy-start | bytes 52
  28.2 65.1 %all-to-all-start = ((bf16[1024,16,128]{2,1,0:T(8,128)(2,1)}), bf16[1024,16,128]{2,1,0:T(8,128)(2,1)}, u32[]{:S(2)}, u32[]{:S(2)}) async-start(bf16[1024,16,128]{2,1,0:T(8,128)(2,1)} %copy.20), calls=%async_computation | async-start | bytes 8388608 | tf_op jit(solution)/shard_map/all_to_all | solution.py:85
  161.9 23.9 %copy-start = (bf16[16,1024,64]{1,2,0:T(8,128)(2,1)S(1)}, bf16[16,1024,64]{1,2,0:T(8,128)(2,1)}, u32[]{:S(2)}) copy-start(bf16[16,1024,64]{1,2,0:T(8,128)(2,1)} %get-tuple-element.7) | copy-start | bytes 6291460
  161.9 23.9 %copy-start.1 = (bf16[16,1024,64]{1,2,0:T(8,128)(2,1)S(1)}, bf16[16,1024,64]{1,2,0:T(8,128)(2,1)}, u32[]{:S(2)}) copy-start(bf16[16,1024,64]{1,2,0:T(8,128)(2,1)} %get-tuple-element.8) | copy-start | bytes 6291460
